TPU v7x, 128 devices: a whole 4x4x4 slice. The times are simulated.
128 devices in a mesh: lat: 16 (over x, y), var: 8 (over z, core).
Axes of the slice: x: 4, y: 4, z: 4, core: 2. Of those that a mesh axis runs over, the one named last changes fastest.
Arguments:
- patches: bfloat16 [96, 192, 1024], P('lat', 'var'), may hold values from -6 to 6
- norm_gain: float32 [1024], replicated, may hold values from 0.25 to 1.75
- input_proj: bfloat16 [1024, 3072], replicated, may hold values from -7 to 7
- output_proj: bfloat16 [1024, 1024], replicated, may hold values from -0.1875 to 0.1875
- level_scale: float32 [40, 1024], P('var'), may hold values from 0.1 to 1.9
- level_shift: float32 [40, 1024], P('var'), may hold values from -3 to 3
- head_weight: bfloat16 [40, 1024, 320], P('var', 'lat'), may hold values from -0.1875 to 0.1875
- targets: bfloat16 [40, 96, 192, 320], P('var', 'lat'), may hold values from -6 to 6
- level_counts: int32 [4], replicated, may hold values from 13 to 37
- tile_dataset: int32 [16, 8], P('lat'), may hold values from 0 to 3
- slot_level: int32 [40], P('var'), may hold values from 0 to 39, as said below
Outputs:
- latent: bfloat16 [96, 192, 1024], P('lat', 'var')
- grad_latent: bfloat16 [96, 192, 1024], P('lat', 'var')
- grad_head: float32 [40, 1024, 320], P('var', 'lat')
Inputs may be any that keep to these rules, and one draw needn't show every extreme that they name: `slot_level`: for each j, slots j * 5 to (j + 1) * 5 - 1 hold the levels j * 5 to (j + 1) * 5 - 1 in some order.
All inputs are finite; a program needn't handle non-finite values.
Results may differ from a plain program's by a relative error of at most 0.012.
Values may be sent and summed in bfloat16 or wider, within the bound.
A program may use at most 128 MiB of HBM per device.

v0:
```python
import math
import jax
import jax.numpy as jnp
from jax import lax
from jax.sharding import PartitionSpec as P

HEADS = 16
WH = 6
WW = 12
EPS = 1e-05


def padded(array, sides, width, wrap):
    for axis, dim in sides:
        size, length = (lax.axis_size(axis), array.shape[dim])
        up = [(i, (i + 1) % size) for i in range(size if wrap else size - 1)]
        down = [(j, i) for i, j in up]
        last = lax.slice_in_dim(array, length - width, length, axis=dim)
        initial = lax.slice_in_dim(array, 0, width, axis=dim)
        before = lax.ppermute(last, axis, up)
        after = lax.ppermute(initial, axis, down)
        array = jnp.concatenate([before, array, after], axis=dim)
    return array


def layer_norm(values, gain):
    wide = values.astype(jnp.float32)
    average = jnp.mean(wide, axis=-1, keepdims=True)
    centred = wide - average
    variance = jnp.mean(centred * centred, axis=-1, keepdims=True)
    return (centred * lax.rsqrt(variance + EPS) * gain).astype(jnp.bfloat16)


def window_attention(query_ext, keyval, row_valid, heads):
    ext_rows, ext_cols, width = query_ext.shape
    head_size = width // heads
    win_rows = ext_rows // WH
    win_cols = ext_cols // WW

    def split(values, parts):
        shaped = values.reshape(win_rows, WH, win_cols, WW, parts, heads, head_size)
        return shaped.transpose(0, 2, 1, 3, 4, 5, 6).reshape(
            win_rows * win_cols, WH * WW, parts, heads, head_size
        )

    query_win = split(query_ext, 1)[:, :, 0]
    pairs = split(keyval, 2)
    key_win = pairs[:, :, 0]
    value_win = pairs[:, :, 1]
    key_mask = jnp.broadcast_to(
        row_valid.reshape(win_rows, 1, WH, 1), (win_rows, win_cols, WH, WW)
    ).reshape(win_rows * win_cols, WH * WW)
    scores = jnp.einsum(
        "wqhd,wkhd->whqk", query_win, key_win, preferred_element_type=jnp.float32
    ) / math.sqrt(head_size)
    scores = jnp.where(key_mask[:, None, None, :], scores, -jnp.inf)
    peak = jnp.max(scores, axis=-1, keepdims=True)
    weights = jnp.exp(scores - peak)
    probs = (weights / jnp.sum(weights, axis=-1, keepdims=True)).astype(jnp.bfloat16)
    mixed = jnp.einsum("whqk,wkhd->wqhd", probs, value_win, preferred_element_type=jnp.float32)
    return (
        mixed.reshape(win_rows, win_cols, WH, WW, width)
        .transpose(0, 2, 1, 3, 4)
        .reshape(ext_rows, ext_cols, width)
    )


def slot_terms(piece, target_rows, live_cols, level_scale, level_shift, heads_full):
    piece_wide = piece.astype(jnp.float32)
    rows = (
        piece_wide[None] * level_scale[:, None, None, :] + level_shift[:, None, None, :]
    ).astype(jnp.bfloat16)
    predicted = jnp.einsum("krnd,kdo->krno", rows, heads_full, preferred_element_type=jnp.float32)
    errors = ((predicted - target_rows.astype(jnp.float32)) * live_cols[:, None, :, None]).astype(
        jnp.bfloat16
    )
    back_grad = jnp.einsum("krno,kdo->krnd", errors, heads_full, preferred_element_type=jnp.float32)
    piece_grad = jnp.sum(back_grad * level_scale[:, None, None, :], axis=0)
    head_add = jnp.einsum("krnd,krno->dko", rows, errors, preferred_element_type=jnp.float32)
    return (piece_grad, head_add)


def local(
    patches,
    norm_gain,
    input_proj,
    output_proj,
    level_scale,
    level_shift,
    head_weight,
    targets,
    level_counts,
    tile_dataset,
    slot_level,
):
    band_rows, band_cols, width = patches.shape
    half_rows = WH // 2
    half_cols = WW // 2
    lat_count = lax.axis_size("lat")
    var_count = lax.axis_size("var")
    lat_place = lax.axis_index("lat")
    ext_rows = band_rows + WH
    ext_cols = band_cols + WW
    extended = padded(patches, (("lat", 0),), half_rows, False)
    extended = padded(extended, (("var", 1),), half_cols, True)
    normed_ext = layer_norm(extended, norm_gain)
    keyval = jnp.dot(
        normed_ext.reshape(-1, width), input_proj[:, width:], preferred_element_type=jnp.float32
    )
    keyval = keyval.astype(jnp.bfloat16).reshape(ext_rows, ext_cols, 2 * width)
    normed = normed_ext[half_rows : half_rows + band_rows, half_cols : half_cols + band_cols]
    queries = jnp.dot(
        normed.reshape(-1, width), input_proj[:, :width], preferred_element_type=jnp.float32
    )
    queries = queries.astype(jnp.bfloat16).reshape(band_rows, band_cols, width)
    query_ext = jnp.pad(queries, ((half_rows, WH - half_rows), (half_cols, WW - half_cols), (0, 0)))
    global_row = lat_place * band_rows - half_rows + jnp.arange(ext_rows, dtype=jnp.int32)
    row_valid = (global_row >= 0) & (global_row < lat_count * band_rows)
    mixed = window_attention(query_ext, keyval, row_valid, HEADS)
    attn = mixed[half_rows : half_rows + band_rows, half_cols : half_cols + band_cols].astype(
        jnp.bfloat16
    )
    update = jnp.dot(
        attn.reshape(-1, width), output_proj, preferred_element_type=jnp.float32
    ).reshape(band_rows, band_cols, width)
    latent = (patches.astype(jnp.float32) + update).astype(jnp.bfloat16)
    dataset_row = tile_dataset[0]
    dataset_ids = jnp.arange(level_counts.shape[0], dtype=jnp.int32)
    tile_levels = jnp.sum(
        jnp.where(dataset_row[:, None] == dataset_ids[None, :], level_counts[None, :], 0), axis=1
    )
    live_tiles = (slot_level[None, :] < tile_levels[:, None]).astype(jnp.float32)
    heads_full = lax.all_gather(head_weight, "lat", axis=1, tiled=True)
    tile_ids = jnp.arange(var_count, dtype=jnp.int32)
    piece = lax.all_gather(latent, "var", axis=1, tiled=True)
    piece_cols = piece.shape[1]
    column_tile = jnp.arange(piece_cols, dtype=jnp.int32) // band_cols
    onehot = (column_tile[:, None] == tile_ids[None, :]).astype(jnp.float32)
    column_live = jnp.dot(onehot, live_tiles)
    piece_grad, head_add = slot_terms(
        piece, targets, column_live.T, level_scale, level_shift, heads_full
    )
    latent_terms = piece_grad
    latent_terms, head_terms = (latent_terms, head_add)
    grad_latent = lax.psum_scatter(
        latent_terms.astype(jnp.bfloat16), "var", scatter_dimension=1, tiled=True
    )
    head_terms = head_terms * (1.0 / math.sqrt(lat_count * band_rows * var_count * band_cols))
    share_rows = width // lat_count
    mine = lax.psum_scatter(
        head_terms.astype(jnp.bfloat16), "lat", scatter_dimension=0, tiled=True
    ).astype(jnp.float32)
    grad_head = jnp.transpose(mine, (1, 0, 2))
    return (latent, grad_latent, grad_head)


def solution(mesh):
    in_specs = (
        P("lat", "var", None),
        P(),
        P(),
        P(),
        P("var", None),
        P("var", None),
        P("var", "lat", None),
        P("var", "lat", None, None),
        P(),
        P("lat", None),
        P("var"),
    )
    out_specs = (P("lat", "var", None), P("lat", "var", None), P("var", "lat", None))
    return jax.shard_map(local, mesh=mesh, in_specs=in_specs, out_specs=out_specs, check_vma=False)
```

profile of v0, /device:TPU:0, one launch (start us, length us, event | category | flops | bytes accessed | tf_op | source)
XLA Modules:
  0.0 313.8 jit_solution(12802649083848093492)
XLA Ops:
  7.2 1.1 fusion.61
  8.4 3.6 %collective-permute-start = (bf16[3,24,1024]{2,1,0:T(8,128)(2,1)S(1)}, bf16[3,24,1024]{2,1,0:T(8,128)(2,1)S(1)}, u32[]{:S(2)}, u32[]{:S(2)}) collective-permute-start(bf16[3,24,1024]{2,1,0:T(8,128)(2,1)S(1)} %get-tuple-element.25), channel_id=1, source_target_pairs={{0,8},{8,16},{16,24},{24,32},{32,40},{40,48},{48,56},{56,64},{64,7... | collective-permute-start | bytes 442376 | tf_op jit(solution)/shard_map/ppermute | solution.py:20
  12.0 1.3 collective-permute-start.1
  13.3 1.8 collective-permute-done
  15.0 1.0 constant_dynamic-update-slice_fusion.1
  16.0 3.1 collective-permute-done.1
  19.3 2.9 collective-permute-start.3
  22.3 0.1 broadcast_in_dim.29
  22.4 3.2 %collective-permute-done.2 = bf16[12,6,1024]{2,1,0:T(8,128)(2,1)S(1)} collective-permute-done((bf16[12,6,1024]{2,1,0:T(8,128)(2,1)S(1)}, bf16[12,6,1024]{2,1,0:T(8,128)(2,1)S(1)}, u32[]{:S(2)}, u32[]{:S(2)}) %collective-permute-start.2) | collective-permute-done | bytes 147488 | tf_op jit(solution)/shard_map/ppermute | solution.py:20
  25.6 0.4 fusion.58
  26.1 1.8 multiply_reduce_fusion.1
  28.1 1.6 maximum_convert_fusion
  29.7 2.7 reshape.102
  32.4 1.3 fusion.50
  33.7 2.1 fusion.40
  35.8 0.2 pad.4
  35.9 2.1 reshape.99
  38.0 3.2 %copy.48 = bf16[2,3,6,12,1,16,64]{6,5,3,2,1,0,4:T(8,128)(2,1)} copy(bf16[2,3,6,12,1,16,64]{6,5,3,1,2,0,4:T(8,128)(2,1)} %bitcast.58) | data formatting | bytes 1769472 | tf_op jit(solution)/shard_map/transpose | solution.py:42
  41.2 5.5 %fusion.15 = bf16[432,2048]{1,0:T(8,128)(2,1)} fusion(bf16[1024,3072]{1,0:T(8,128)(2,1)} %param.13, f32[432,1024]{1,0:T(8,128)S(1)} %copy-done.2, f32[1024]{0:T(1024)S(1)} %copy-done.4, f32[432]{0:T(512)S(1)} %rsqrt.13, f32[432]{0:T(512)S(1)} %div.33), kind=kOutput, calls=%fused_computation.22 | convolution fusion | flops 1814593536 | bytes 7740800 | tf_op jit(solution)/shard_map/dot_general | solution.py:107
  46.8 6.4 %reshape_reshape.3 = bf16[2,6,3,12,2,16,64]{6,5,4,3,2,1,0:T(8,128)(2,1)} reshape(bf16[432,2048]{1,0:T(8,128)(2,1)} %fusion.15) | data formatting | bytes 3538944 | tf_op jit(solution)/shard_map/reshape;reshape | solution.py:41
  53.1 2.6 copy.46
  55.7 2.6 fusion.59
  58.3 4.0 %copy.61 = bf16[6,72,1,16,64]{1,4,3,0,2:T(8,128)(2,1)} copy(bf16[6,72,1,16,64]{4,3,2,1,0:T(8,128)(2,1)} %get-tuple-element.18) | data formatting | bytes 1769472
  62.4 4.0 %copy.62 = bf16[6,72,1,16,64]{1,4,3,0,2:T(8,128)(2,1)} copy(bf16[6,72,1,16,64]{4,3,2,1,0:T(8,128)(2,1)} %get-tuple-element.19) | data formatting | bytes 1769472
  66.4 3.1 fusion.25
  69.5 1.8 fusion.62
  71.3 1.9 fusion.34
  73.2 4.0 %copy.52 = bf16[6,72,16,64]{3,2,1,0:T(8,128)(2,1)} copy(bf16[6,72,16,64]{1,3,2,0:T(8,128)(2,1)} %fusion.34) | data formatting | bytes 1769472 | tf_op jit(solution)/shard_map/whqk,wkhd->wqhd/transpose | solution.py:60
  77.2 3.9 %reshape.100 = bf16[2,3,6,12,1024]{4,3,2,1,0:T(8,128)(2,1)} reshape(bf16[6,72,16,64]{3,2,1,0:T(8,128)(2,1)} %copy.52) | data formatting | bytes 1769472 | tf_op jit(solution)/shard_map/reshape | solution.py:62
  81.1 1.4 copy.53
  82.5 1.0 reshape.101
  83.6 2.3 fusion.43
  85.9 0.7 all-gather.5.cloned.1.call-update
  86.8 0.2 fusion.52
  87.1 28.5 %all-gather.3.cloned.1.call-done = bf16[6,192,1024]{2,1,0:T(8,128)(2,1)} async-done(((bf16[6,24,1024]{2,1,0:T(8,128)(2,1)}), bf16[6,192,1024]{2,1,0:T(8,128)(2,1)}) %all-gather.3.cloned.1.call-update) | async-done | bytes 2359312 | tf_op jit(solution)/shard_map/all_gather | solution.py:135
  115.6 4.3 %convert_element_type.67 = f32[6,192,1024]{2,1,0:T(8,128)} convert(bf16[6,192,1024]{2,1,0:T(8,128)(2,1)} %all-gather.3.cloned.1.call-done) | non-fusion elementwise | flops 1179648 | bytes 7077888 | tf_op jit(solution)/shard_map/convert_element_type | solution.py:69
  119.9 48.6 %all-gather.5.cloned.1.call-done = bf16[5,1024,320]{2,1,0:T(8,128)(2,1)} async-done(((bf16[5,64,320]{2,1,0:T(8,128)(2,1)}), bf16[5,1024,320]{2,1,0:T(8,128)(2,1)}) %all-gather.5.cloned.1.call-update) | async-done | bytes 3276816 | tf_op jit(solution)/shard_map/all_gather | solution.py:133
  168.5 10.6 %multiply_convert_fusion = bf16[5,6,192,320]{3,2,1,0:T(8,128)(2,1)S(1)} fusion(bf16[5,6,192,320]{3,2,1,0:T(8,128)(2,1)} %param.18, f32[5,192]{1,0:T(8,128)S(1)} %fusion.52, bf16[5,1024,320]{2,1,0:T(8,128)(2,1)} %all-gather.5.cloned.1.call-done, f32[5,1024]{1,0:T(8,128)S(1)} %copy-done.7, f32[5,1024]{1,0:T(8,128)S(1)} %copy-done.6, ...), kind=kOutput, calls=%fused_computation.11 | convolution fusion | flops 3799941120 | bytes 15412992 | tf_op jit(solution)/shard_map/krnd,kdo->krno/dot_general | solution.py:73
  179.2 7.2 %multiply_reduce_fusion = bf16[6,192,1024]{2,1,0:T(8,128)(2,1)S(1)} fusion(f32[5,1024]{1,0:T(8,128)S(1)} %copy-done.6, bf16[5,6,192,320]{3,2,1,0:T(8,128)(2,1)S(1)} %multiply_convert_fusion, bf16[5,1024,320]{2,1,0:T(8,128)(2,1)S(1)} %copy-done.5), kind=kOutput, calls=%fused_computation.1 | convolution fusion | flops 3785490432 | bytes 9342976 | tf_op jit(solution)/shard_map/krno,kdo->krnd/dot_general | solution.py:77
  186.4 1.7 copy.63
  188.2 9.3 %fusion.14 = bf16[1024,5,320]{0,2,1:T(8,128)(2,1)} fusion(bf16[5,6,192,320]{3,2,1,0:T(8,128)(2,1)} %copy-done.11, f32[5,1024]{1,0:T(8,128)S(1)} %copy-done.7, f32[5,1024]{1,0:T(8,128)S(1)} %copy-done.6, f32[6,192,1024]{2,1,0:T(8,128)} %convert_element_type.67), kind=kOutput, calls=%fused_computation.21 | convolution fusion | flops 3795845120 | bytes 11722752 | tf_op jit(solution)/shard_map/krnd,krno->dko/dot_general | solution.py:79
  197.5 8.2 %copy.54 = bf16[1024,5,320]{2,1,0:T(8,128)(2,1)} copy(bf16[1024,5,320]{0,2,1:T(8,128)(2,1)} %fusion.14) | data formatting | bytes 6553600 | tf_op jit(solution)/shard_map/convert_element_type | solution.py:151
  205.7 16.5 %reduce-scatter.7.cloned.1.call-done = bf16[24,6144]{1,0:T(8,128)(2,1)} async-done(((bf16[192,6144]{1,0:T(8,128)(2,1)}), bf16[24,6144]{1,0:T(8,128)(2,1)}) %reduce-scatter.7.cloned.1.call-update) | async-done | bytes 294928
  222.2 1.3 reshape.107
  223.5 0.9 copy.60
  224.4 80.9 %reduce-scatter.5.cloned.1.call-done = bf16[64,5,320]{2,1,0:T(8,128)(2,1)} async-done(((bf16[1024,5,320]{2,1,0:T(8,128)(2,1)}), bf16[64,5,320]{2,1,0:T(8,128)(2,1)}) %reduce-scatter.5.cloned.1.call-update) | async-done | bytes 204816 | tf_op jit(solution)/shard_map/reduce_scatter | solution.py:150
  305.3 1.0 convert_bitcast_fusion
  306.4 0.9 copy.55
  (45 shorter events, 0.8 us)
Async XLA Ops:
  7.2 76.4 %copy-start = (bf16[1024,1024]{1,0:T(8,128)(2,1)S(1)}, bf16[1024,1024]{1,0:T(8,128)(2,1)}, u32[]{:S(2)}) copy-start(bf16[1024,1024]{1,0:T(8,128)(2,1)} %param.14) | copy-start | bytes 6291460
  7.2 108.4 %all-gather.3.cloned.1.call-start = ((), (), s32[]{:S(2)}) async-start(), calls=%async_computation.2 | async-start | bytes 2654208 | tf_op jit(solution)/shard_map/all_gather | solution.py:135
  8.4 6.7 %collective-permute-start = (bf16[3,24,1024]{2,1,0:T(8,128)(2,1)S(1)}, bf16[3,24,1024]{2,1,0:T(8,128)(2,1)S(1)}, u32[]{:S(2)}, u32[]{:S(2)}) collective-permute-start(bf16[3,24,1024]{2,1,0:T(8,128)(2,1)S(1)} %get-tuple-element.25), channel_id=1, source_target_pairs={{0,8},{8,16},{16,24},{24,32},{32,40},{40,48},{48,56},{56,64},{64,7... | collective-permute-start | bytes 442376 | tf_op jit(solution)/shard_map/ppermute | solution.py:20
  12.0 7.2 %collective-permute-start.1 = (bf16[3,24,1024]{2,1,0:T(8,128)(2,1)S(1)}, bf16[3,24,1024]{2,1,0:T(8,128)(2,1)S(1)}, u32[]{:S(2)}, u32[]{:S(2)}) collective-permute-start(bf16[3,24,1024]{2,1,0:T(8,128)(2,1)S(1)} %get-tuple-element.24), channel_id=1, source_target_pairs={{8,0},{16,8},{24,16},{32,24},{40,32},{48,40},{56,48},{64,56},{72,6... | collective-permute-start | bytes 442376 | tf_op jit(solution)/shard_map/ppermute | solution.py:21
  19.2 6.3 %collective-permute-start.2 = (bf16[12,6,1024]{2,1,0:T(8,128)(2,1)S(1)}, bf16[12,6,1024]{2,1,0:T(8,128)(2,1)S(1)}, u32[]{:S(2)}, u32[]{:S(2)}) collective-permute-start(bf16[12,6,1024]{2,1,0:T(8,128)(2,1)S(1)} %get-tuple-element.22), channel_id=1, source_target_pairs={{0,1},{1,2},{2,3},{3,4},{4,5},{5,6},{6,7},{7,0},{8,9},{9,10},{10,1... | collective-permute-start | bytes 442376 | tf_op jit(solution)/shard_map/ppermute | solution.py:20
  19.3 6.3 %collective-permute-start.3 = (bf16[12,6,1024]{2,1,0:T(8,128)(2,1)S(1)}, bf16[12,6,1024]{2,1,0:T(8,128)(2,1)S(1)}, u32[]{:S(2)}, u32[]{:S(2)}) collective-permute-start(bf16[12,6,1024]{2,1,0:T(8,128)(2,1)S(1)} %get-tuple-element.23), channel_id=1, source_target_pairs={{1,0},{2,1},{3,2},{4,3},{5,4},{6,5},{7,6},{0,7},{9,8},{10,9},{11,1... | collective-permute-start | bytes 442376 | tf_op jit(solution)/shard_map/ppermute | solution.py:21
  27.9 4.5 %copy-start.4 = (f32[1024]{0:T(1024)S(1)}, f32[1024]{0:T(1024)}, u32[]{:S(2)}) copy-start(f32[1024]{0:T(1024)} %param.12) | copy-start | bytes 12292
  38.0 3.2 %copy-start.2 = (f32[432,1024]{1,0:T(8,128)S(1)}, f32[432,1024]{1,0:T(8,128)}, u32[]{:S(2)}) copy-start(f32[432,1024]{1,0:T(8,128)} %reshape.102) | copy-start | bytes 5308420
  69.5 1.8 copy-start.3
  82.5 4.2 %copy-start.8 = (s32[4]{0:T(128)S(1)}, s32[4]{0:T(128)}, u32[]{:S(2)}) copy-start(s32[4]{0:T(128)} %param.19) | copy-start | bytes 52
  82.5 4.2 %copy-start.9 = (s32[1,8]{1,0:T(1,128)S(1)}, s32[1,8]{1,0:T(1,128)}, u32[]{:S(2)}) copy-start(s32[1,8]{1,0:T(1,128)} %param.20) | copy-start | bytes 100
  82.5 4.3 %copy-start.10 = (s32[5]{0:T(128)S(1)}, s32[5]{0:T(128)}, u32[]{:S(2)}) copy-start(s32[5]{0:T(128)} %param.21) | copy-start | bytes 64
  85.9 82.6 %all-gather.5.cloned.1.call-start = ((), (), s32[]{:S(2)}) async-start(), calls=%async_computation.3 | async-start | bytes 4177920 | tf_op jit(solution)/shard_map/all_gather | solution.py:133
  86.6 135.5 %reduce-scatter.7.cloned.1.call-start = ((), (), s32[]{:S(2)}) async-start(), calls=%async_computation.5 | async-start | bytes 2654208
  87.1 81.5 %copy-start.6 = (f32[5,1024]{1,0:T(8,128)S(1)}, f32[5,1024]{1,0:T(8,128)}, u32[]{:S(2)}) copy-start(f32[5,1024]{1,0:T(8,128)} %param.15) | copy-start | bytes 61444
  87.1 81.5 %copy-start.7 = (f32[5,1024]{1,0:T(8,128)S(1)}, f32[5,1024]{1,0:T(8,128)}, u32[]{:S(2)}) copy-start(f32[5,1024]{1,0:T(8,128)} %param.16) | copy-start | bytes 61444
  168.5 10.6 %copy-start.5 = (bf16[5,1024,320]{2,1,0:T(8,128)(2,1)S(1)}, bf16[5,1024,320]{2,1,0:T(8,128)(2,1)}, u32[]{:S(2)}) copy-start(bf16[5,1024,320]{2,1,0:T(8,128)(2,1)} %all-gather.5.cloned.1.call-done) | copy-start | bytes 9830404
  179.2 7.2 %copy-start.11 = (bf16[5,6,192,320]{3,2,1,0:T(8,128)(2,1)}, bf16[5,6,192,320]{3,2,1,0:T(8,128)(2,1)S(1)}, u32[]{:S(2)}) copy-start(bf16[5,6,192,320]{3,2,1,0:T(8,128)(2,1)S(1)} %multiply_convert_fusion) | copy-start | bytes 11059204
  188.1 117.2 %reduce-scatter.5.cloned.1.call-start = ((), (), s32[]{:S(2)}) async-start(), calls=%async_computation.4 | async-start | bytes 6684672 | tf_op jit(solution)/shard_map/reduce_scatter | solution.py:150
  205.7 101.6 %copy-start.1 = (bf16[1024,1024]{1,0:T(8,128)(2,1)S(1)}, bf16[1024,1024]{1,0:T(8,128)(2,1)}, u32[]{:S(2)}) copy-start(bf16[1024,1024]{1,0:T(8,128)(2,1)} %param.14) | copy-start | bytes 6291460
Sparse Core Ops, SparseCore 0:
  86.0 29.4 all-gather.2
  117.7 50.7 all-gather.4
  188.2 33.9 reduce-scatter.6
  225.5 79.7 reduce-scatter.4
where the time goes:
time: 315 us; the launch traced here: 314 us
  waiting for transfers between devices  183 us (58%)
  local copies, waits for them, and re-layouts  53.8 us (17%)
  matrix products  42.2 us (13%)
  between operations  14 us (4%)
  other arithmetic  12.5 us (4%)
  starting transfers between devices  7.98 us (3%)
    reduce_scatter x1, waiting for transfers between devices, local(): lax.psum_scatter(head_terms.astype(jnp.bfloat16), 'lat', scatter_dimensio...  80.9 us
    all_gather x1, waiting for transfers between devices, local(): heads_full = lax.all_gather(head_weight, 'lat', axis=1, tiled=True)  48.6 us
    all_gather x1, waiting for transfers between devices, local(): piece = lax.all_gather(latent, 'var', axis=1, tiled=True)  28.5 us
    unnamed x5, waiting for transfers between devices  17.3 us
    unnamed x32, local copies, waits for them, and re-layouts  13.9 us
    dot_general x1, matrix products, slot_terms(): jnp.einsum('krnd,kdo->krno', rows, heads_full, preferred_element_type=jnp...  10.6 us
    dot_general x1, matrix products, slot_terms(): jnp.einsum('krnd,krno->dko', rows, errors, preferred_element_type=jnp.flo...  9.29 us
    another operation x2, local copies, waits for them, and re-layouts, split(): shaped = values.reshape(win_rows, WH, win_cols, WW, parts, heads, head_size)  8.98 us
  transfers between devices with their start and end apart: 8, of which 7 were waited for; matrix products, arithmetic and copies ran while one was open for 8% of the time, Pallas kernels for 0%

commit v1 on v0

--- a/solution.py
+++ b/solution.py
@@ -8,6 +8,19 @@
 WH = 6
 WW = 12
 EPS = 1e-05
+
+
+def ring_gather(value, axis, dim):
+    ways = lax.axis_size(axis)
+    up = [(d, (d + 1) % ways) for d in range(ways)]
+    down = [(d, (d - 1) % ways) for d in range(ways)]
+    earlier, later = ([value], [value])
+    for _ in range(ways // 2):
+        earlier.append(lax.ppermute(earlier[-1], axis, up))
+    for _ in range((ways - 1) // 2):
+        later.append(lax.ppermute(later[-1], axis, down))
+    line = jnp.concatenate([*earlier[::-1], *later[1:]], axis=dim)
+    return jnp.roll(line, (lax.axis_index(axis) - ways // 2) * value.shape[dim], axis=dim)
 
 
 def padded(array, sides, width, wrap):
@@ -130,7 +143,7 @@
         jnp.where(dataset_row[:, None] == dataset_ids[None, :], level_counts[None, :], 0), axis=1
     )
     live_tiles = (slot_level[None, :] < tile_levels[:, None]).astype(jnp.float32)
-    heads_full = lax.all_gather(head_weight, "lat", axis=1, tiled=True)
+    heads_full = ring_gather(head_weight, "lat", 1)
     tile_ids = jnp.arange(var_count, dtype=jnp.int32)
     piece = lax.all_gather(latent, "var", axis=1, tiled=True)
     piece_cols = piece.shape[1]

time: 315 us -> 356 us (1.13)
  starting transfers between devices: 7.98 us -> 45.4 us
  local copies, waits for them, and re-layouts: 53.8 us -> 72.6 us
  waiting for transfers between devices: 183 us -> 168 us
    ppermute x0 -> x15, waiting for transfers between devices: none -> 63.5 us  [the longest x8 63.5 us: ring_gather(): earlier.append(lax.ppermute(earlier[-1], axis, up))]
    all_gather x1 -> x0, waiting for transfers between devices: 48.6 us -> none  [local(): heads_full = lax.all_gather(head_weight, 'lat', axis=1, tiled=True)]
    ppermute x0 -> x15, starting transfers between devices: none -> 37.5 us  [the longest x7 35.8 us: ring_gather(): later.append(lax.ppermute(later[-1], axis, down))]
    all_gather x1, waiting for transfers between devices: 28.5 us -> 0.02 us  [local(): piece = lax.all_gather(latent, 'var', axis=1, tiled=True)]
    concatenate x0 -> x1, local copies, waits for them, and re-layouts: none -> 15.2 us  [ring_gather(): jnp.roll(line, (lax.axis_index(axis) - ways // 2) * value.shape[dim], axi...]
    unnamed x32 -> x43, local copies, waits for them, and re-layouts: 13.9 us -> 17.4 us
    unnamed x5 -> x4, waiting for transfers between devices: 17.3 us -> 15.6 us
  transfers between devices with their start and end apart: 8 -> 22, of which waited for: 7 -> 13; matrix products, arithmetic and copies ran while one was open for 8% -> 10% of each run, Pallas kernels for 0% -> 0%
where the time goes in v1:
time: 356 us; the launch traced here: 353 us
  waiting for transfers between devices  168 us (47%)
  local copies, waits for them, and re-layouts  72.6 us (20%)
  starting transfers between devices  45.4 us (13%)
  matrix products  42.6 us (12%)
  between operations  14.1 us (4%)
  other arithmetic  10.5 us (3%)
    reduce_scatter x1, waiting for transfers between devices, local(): lax.psum_scatter(head_terms.astype(jnp.bfloat16), 'lat', scatter_dimensio...  81.1 us
    ppermute x8, waiting for transfers between devices, ring_gather(): earlier.append(lax.ppermute(earlier[-1], axis, up))  63.5 us
    ppermute x7, starting transfers between devices, ring_gather(): later.append(lax.ppermute(later[-1], axis, down))  35.8 us
    unnamed x43, local copies, waits for them, and re-layouts  17.4 us
    unnamed x4, waiting for transfers between devices  15.6 us
    concatenate x1, local copies, waits for them, and re-layouts, ring_gather(): jnp.roll(line, (lax.axis_index(axis) - ways // 2) * value.shape[dim], axi...  15.2 us
    dot_general x1, matrix products, slot_terms(): jnp.einsum('krnd,kdo->krno', rows, heads_full, preferred_element_type=jnp...  10.9 us
    dot_general x1, matrix products, slot_terms(): jnp.einsum('krnd,krno->dko', rows, errors, preferred_element_type=jnp.flo...  9.27 us
  transfers between devices with their start and end apart: 22, of which 13 were waited for; matrix products, arithmetic and copies ran while one was open for 10% of the time, Pallas kernels for 0%

profile of v1, /device:TPU:0, one launch (start us, length us, event | category | flops | bytes accessed | tf_op | source)
XLA Modules:
  0.0 353.5 jit_solution(9327504747094295079)
XLA Ops:
  8.4 3.6 %collective-permute-start = (bf16[3,24,1024]{2,1,0:T(8,128)(2,1)S(1)}, bf16[3,24,1024]{2,1,0:T(8,128)(2,1)S(1)}, u32[]{:S(2)}, u32[]{:S(2)}) collective-permute-start(bf16[3,24,1024]{2,1,0:T(8,128)(2,1)S(1)} %get-tuple-element.25), channel_id=1, source_target_pairs={{0,8},{8,16},{16,24},{24,32},{32,40},{40,48},{48,56},{56,64},{64,7... | collective-permute-start | bytes 442376 | tf_op jit(solution)/shard_map/ppermute | solution.py:33
  13.3 1.8 collective-permute-done
  16.0 3.1 collective-permute-done.1
  19.3 2.9 collective-permute-start.3
  22.4 3.2 collective-permute-done.2
  26.1 1.8 multiply_reduce_fusion.1
  28.1 1.6 maximum_convert_fusion
  29.7 2.7 reshape.102
  33.7 2.1 fusion.42
  35.9 2.1 reshape.99
  38.1 3.2 copy.64
  41.3 5.5 %fusion.17 = bf16[432,2048]{1,0:T(8,128)(2,1)} fusion(bf16[1024,3072]{1,0:T(8,128)(2,1)} %param.13, f32[432,1024]{1,0:T(8,128)S(1)} %copy-done.4, f32[1024]{0:T(1024)S(1)} %copy-done.10, f32[432]{0:T(512)S(1)} %rsqrt.13, f32[432]{0:T(512)S(1)} %div.33), kind=kOutput, calls=%fused_computation.24 | convolution fusion | flops 1814593536 | bytes 7740800 | tf_op jit(solution)/shard_map/dot_general | solution.py:120
  46.8 6.4 %reshape_reshape.3 = bf16[2,6,3,12,2,16,64]{6,5,4,3,2,1,0:T(8,128)(2,1)} reshape(bf16[432,2048]{1,0:T(8,128)(2,1)} %fusion.17) | data formatting | bytes 3538944 | tf_op jit(solution)/shard_map/reshape;reshape | solution.py:54
  53.1 2.6 copy.62
  55.8 2.6 fusion.63
  58.4 4.1 %copy.81 = bf16[6,72,1,16,64]{1,4,3,0,2:T(8,128)(2,1)} copy(bf16[6,72,1,16,64]{4,3,2,1,0:T(8,128)(2,1)} %get-tuple-element.18) | data formatting | bytes 1769472
  62.4 4.0 %copy.82 = bf16[6,72,1,16,64]{1,4,3,0,2:T(8,128)(2,1)} copy(bf16[6,72,1,16,64]{4,3,2,1,0:T(8,128)(2,1)} %get-tuple-element.19) | data formatting | bytes 1769472
  66.5 3.1 fusion.27
  69.6 1.8 fusion.66
  71.4 1.9 fusion.36
  73.3 4.0 %copy.68 = bf16[6,72,16,64]{3,2,1,0:T(8,128)(2,1)} copy(bf16[6,72,16,64]{1,3,2,0:T(8,128)(2,1)} %fusion.36) | data formatting | bytes 1769472 | tf_op jit(solution)/shard_map/whqk,wkhd->wqhd/transpose | solution.py:73
  77.3 3.9 %reshape.100 = bf16[2,3,6,12,1024]{4,3,2,1,0:T(8,128)(2,1)} reshape(bf16[6,72,16,64]{3,2,1,0:T(8,128)(2,1)} %copy.68) | data formatting | bytes 1769472 | tf_op jit(solution)/shard_map/reshape | solution.py:75
  83.7 2.3 fusion.45
  86.4 1.6 collective-permute-start.4
  88.0 3.8 %collective-permute-start.12 = (bf16[5,64,320]{1,2,0:T(8,128)(2,1)S(1)}, bf16[5,64,320]{1,2,0:T(8,128)(2,1)S(1)}, u32[]{:S(2)}, u32[]{:S(2)}) collective-permute-start(bf16[5,64,320]{1,2,0:T(8,128)(2,1)S(1)} %copy.70), channel_id=1, source_target_pairs={{0,120},{8,0},{16,8},{24,16},{32,24},{40,32},{48,40},{56,48},{64,5... | collective-permute-start | bytes 614408 | tf_op jit(solution)/shard_map/ppermute | solution.py:21
  91.8 10.2 %collective-permute-done.4 = bf16[5,64,320]{1,2,0:T(8,128)(2,1)S(1)} collective-permute-done((bf16[5,64,320]{1,2,0:T(8,128)(2,1)S(1)}, bf16[5,64,320]{1,2,0:T(8,128)(2,1)S(1)}, u32[]{:S(2)}, u32[]{:S(2)}) %collective-permute-start.4) | collective-permute-done | bytes 204832 | tf_op jit(solution)/shard_map/ppermute | solution.py:19
  102.0 5.3 %collective-permute-start.13 = (bf16[5,64,320]{1,2,0:T(8,128)(2,1)S(1)}, bf16[5,64,320]{1,2,0:T(8,128)(2,1)S(1)}, u32[]{:S(2)}, u32[]{:S(2)}) collective-permute-start(bf16[5,64,320]{1,2,0:T(8,128)(2,1)S(1)} %collective-permute-done.12), channel_id=1, source_target_pairs={{0,120},{8,0},{16,8},{24,16},{32,24},{40,32},{48,40},{56,48},{64,5... | collective-permute-start | bytes 614408 | tf_op jit(solution)/shard_map/ppermute | solution.py:21
  107.3 9.3 %collective-permute-done.5 = bf16[5,64,320]{1,2,0:T(8,128)(2,1)S(1)} collective-permute-done((bf16[5,64,320]{1,2,0:T(8,128)(2,1)S(1)}, bf16[5,64,320]{1,2,0:T(8,128)(2,1)S(1)}, u32[]{:S(2)}, u32[]{:S(2)}) %collective-permute-start.5) | collective-permute-done | bytes 204832 | tf_op jit(solution)/shard_map/ppermute | solution.py:19
  116.6 5.3 %collective-permute-start.14 = (bf16[5,64,320]{1,2,0:T(8,128)(2,1)S(1)}, bf16[5,64,320]{1,2,0:T(8,128)(2,1)S(1)}, u32[]{:S(2)}, u32[]{:S(2)}) collective-permute-start(bf16[5,64,320]{1,2,0:T(8,128)(2,1)S(1)} %collective-permute-done.13), channel_id=1, source_target_pairs={{0,120},{8,0},{16,8},{24,16},{32,24},{40,32},{48,40},{56,48},{64,5... | collective-permute-start | bytes 614408 | tf_op jit(solution)/shard_map/ppermute | solution.py:21
  122.0 8.4 %collective-permute-done.6 = bf16[5,64,320]{1,2,0:T(8,128)(2,1)S(1)} collective-permute-done((bf16[5,64,320]{1,2,0:T(8,128)(2,1)S(1)}, bf16[5,64,320]{1,2,0:T(8,128)(2,1)S(1)}, u32[]{:S(2)}, u32[]{:S(2)}) %collective-permute-start.6) | collective-permute-done | bytes 204832 | tf_op jit(solution)/shard_map/ppermute | solution.py:19
  130.4 5.3 %collective-permute-start.15 = (bf16[5,64,320]{1,2,0:T(8,128)(2,1)S(1)}, bf16[5,64,320]{1,2,0:T(8,128)(2,1)}, u32[]{:S(2)}, u32[]{:S(2)}) collective-permute-start(bf16[5,64,320]{1,2,0:T(8,128)(2,1)S(1)} %collective-permute-done.14), channel_id=1, source_target_pairs={{0,120},{8,0},{16,8},{24,16},{32,24},{40,32},{48,40},{56,48},{64,5... | collective-permute-start | bytes 614408 | tf_op jit(solution)/shard_map/ppermute | solution.py:21
  135.8 7.5 %collective-permute-done.7 = bf16[5,64,320]{1,2,0:T(8,128)(2,1)S(1)} collective-permute-done((bf16[5,64,320]{1,2,0:T(8,128)(2,1)S(1)}, bf16[5,64,320]{1,2,0:T(8,128)(2,1)S(1)}, u32[]{:S(2)}, u32[]{:S(2)}) %collective-permute-start.7) | collective-permute-done | bytes 204832 | tf_op jit(solution)/shard_map/ppermute | solution.py:19
  143.3 5.3 %collective-permute-start.16 = (bf16[5,64,320]{1,2,0:T(8,128)(2,1)}, bf16[5,64,320]{1,2,0:T(8,128)(2,1)}, u32[]{:S(2)}, u32[]{:S(2)}) collective-permute-start(bf16[5,64,320]{1,2,0:T(8,128)(2,1)} %collective-permute-done.15), channel_id=1, source_target_pairs={{0,120},{8,0},{16,8},{24,16},{32,24},{40,32},{48,40},{56,48},{64,5... | collective-permute-start | bytes 614408 | tf_op jit(solution)/shard_map/ppermute | solution.py:21
  148.6 6.7 %collective-permute-done.8 = bf16[5,64,320]{1,2,0:T(8,128)(2,1)} collective-permute-done((bf16[5,64,320]{1,2,0:T(8,128)(2,1)S(1)}, bf16[5,64,320]{1,2,0:T(8,128)(2,1)}, u32[]{:S(2)}, u32[]{:S(2)}) %collective-permute-start.8) | collective-permute-done | bytes 204832 | tf_op jit(solution)/shard_map/ppermute | solution.py:19
  155.4 5.3 %collective-permute-start.17 = (bf16[5,64,320]{1,2,0:T(8,128)(2,1)}, bf16[5,64,320]{1,2,0:T(8,128)(2,1)S(1)}, u32[]{:S(2)}, u32[]{:S(2)}) collective-permute-start(bf16[5,64,320]{1,2,0:T(8,128)(2,1)} %collective-permute-done.16), channel_id=1, source_target_pairs={{0,120},{8,0},{16,8},{24,16},{32,24},{40,32},{48,40},{56,48},{64,5... | collective-permute-start | bytes 614408 | tf_op jit(solution)/shard_map/ppermute | solution.py:21
  160.7 6.2 %collective-permute-done.9 = bf16[5,64,320]{1,2,0:T(8,128)(2,1)} collective-permute-done((bf16[5,64,320]{1,2,0:T(8,128)(2,1)}, bf16[5,64,320]{1,2,0:T(8,128)(2,1)}, u32[]{:S(2)}, u32[]{:S(2)}) %collective-permute-start.9) | collective-permute-done | bytes 204832 | tf_op jit(solution)/shard_map/ppermute | solution.py:19
  167.8 5.3 %collective-permute-start.18 = (bf16[5,64,320]{1,2,0:T(8,128)(2,1)S(1)}, bf16[5,64,320]{1,2,0:T(8,128)(2,1)S(1)}, u32[]{:S(2)}, u32[]{:S(2)}) collective-permute-start(bf16[5,64,320]{1,2,0:T(8,128)(2,1)S(1)} %collective-permute-done.17), channel_id=1, source_target_pairs={{0,120},{8,0},{16,8},{24,16},{32,24},{40,32},{48,40},{56,48},{64,5... | collective-permute-start | bytes 614408 | tf_op jit(solution)/shard_map/ppermute | solution.py:21
  173.2 5.3 %collective-permute-done.10 = bf16[5,64,320]{1,2,0:T(8,128)(2,1)S(1)} collective-permute-done((bf16[5,64,320]{1,2,0:T(8,128)(2,1)}, bf16[5,64,320]{1,2,0:T(8,128)(2,1)S(1)}, u32[]{:S(2)}, u32[]{:S(2)}) %collective-permute-start.10) | collective-permute-done | bytes 204832 | tf_op jit(solution)/shard_map/ppermute | solution.py:19
  179.9 9.9 %collective-permute-done.11 = bf16[5,64,320]{1,2,0:T(8,128)(2,1)} collective-permute-done((bf16[5,64,320]{1,2,0:T(8,128)(2,1)S(1)}, bf16[5,64,320]{1,2,0:T(8,128)(2,1)}, u32[]{:S(2)}, u32[]{:S(2)}) %collective-permute-start.11) | collective-permute-done | bytes 204832 | tf_op jit(solution)/shard_map/ppermute | solution.py:19
  189.8 15.2 %concatenate.14 = bf16[5,2048,320]{1,2,0:T(8,128)(2,1)} concatenate(bf16[5,64,320]{1,2,0:T(8,128)(2,1)} %collective-permute-done.11, bf16[5,64,320]{1,2,0:T(8,128)(2,1)} %copy-done.6, bf16[5,64,320]{1,2,0:T(8,128)(2,1)} %collective-permute-done.9, bf16[5,64,320]{1,2,0:T(8,128)(2,1)} %collective-permute-done.8, bf16[5,64,320]{1,2,0:T(8,128)(2,1)S(1)} %collective-permute-done.7, ...), dimensions={1} | concatenate | bytes 13107200 | tf_op jit(solution)/shard_map/jit(_roll_dynamic)/concatenate | solution.py:23
  205.1 2.3 convert_element_type.67
  208.6 10.9 %multiply_convert_fusion = bf16[5,6,192,320]{3,2,1,0:T(8,128)(2,1)S(1)} fusion(bf16[5,6,192,320]{3,2,1,0:T(8,128)(2,1)} %param.18, f32[5,192]{1,0:T(8,128)S(1)} %fusion.54, bf16[5,2048,320]{1,2,0:T(8,128)(2,1)S(1)} %copy-done.2, s32[]{:T(128)S(6)} %select_n.32, f32[5,1024]{1,0:T(8,128)S(1)} %copy-done.12, f32[5,1024]{1,0:T(8,128)S(1)} %copy-done.11, ...), kind=kOutput, calls=%fused_computation.11 | convolution fusion | flops 3799941120 | bytes 15441924 | tf_op jit(solution)/shard_map/krnd,kdo->krno/dot_general | solution.py:86
  219.5 7.3 %multiply_reduce_fusion = bf16[6,192,1024]{2,1,0:T(8,128)(2,1)S(1)} fusion(f32[5,1024]{1,0:T(8,128)S(1)} %copy-done.11, bf16[5,6,192,320]{3,2,1,0:T(8,128)(2,1)S(1)} %multiply_convert_fusion, bf16[5,2048,320]{1,2,0:T(8,128)(2,1)S(1)} %copy-done.2, s32[]{:T(128)S(6)} %select_n.32), kind=kOutput, calls=%fused_computation.1 | convolution fusion | flops 3785490432 | bytes 10092548 | tf_op jit(solution)/shard_map/krno,kdo->krnd/dot_general | solution.py:90
  226.9 1.7 copy.83
  228.6 9.3 %fusion.12 = bf16[1024,5,320]{0,2,1:T(8,128)(2,1)} fusion(bf16[5,6,192,320]{3,2,1,0:T(8,128)(2,1)} %copy-done.16, f32[5,1024]{1,0:T(8,128)S(1)} %copy-done.12, f32[5,1024]{1,0:T(8,128)S(1)} %copy-done.11, f32[6,192,1024]{2,1,0:T(8,128)} %copy-done.3), kind=kOutput, calls=%fused_computation.19 | convolution fusion | flops 3795845120 | bytes 11722752 | tf_op jit(solution)/shard_map/krnd,krno->dko/dot_general | solution.py:92
  237.9 8.2 %copy.74 = bf16[1024,5,320]{2,1,0:T(8,128)(2,1)} copy(bf16[1024,5,320]{0,2,1:T(8,128)(2,1)} %fusion.12) | data formatting | bytes 6553600 | tf_op jit(solution)/shard_map/convert_element_type | solution.py:164
  246.2 15.6 %reduce-scatter.7.cloned.1.call-done = bf16[24,6144]{1,0:T(8,128)(2,1)} async-done(((bf16[192,6144]{1,0:T(8,128)(2,1)}), bf16[24,6144]{1,0:T(8,128)(2,1)}) %reduce-scatter.7.cloned.1.call-update) | async-done | bytes 294928
  264.0 81.1 %reduce-scatter.5.cloned.1.call-done = bf16[64,5,320]{2,1,0:T(8,128)(2,1)} async-done(((bf16[1024,5,320]{2,1,0:T(8,128)(2,1)}), bf16[64,5,320]{2,1,0:T(8,128)(2,1)}) %reduce-scatter.5.cloned.1.call-update) | async-done | bytes 204816 | tf_op jit(solution)/shard_map/reduce_scatter | solution.py:163
  (84 shorter events, 16.5 us)
Async XLA Ops:
  7.2 76.6 %copy-start = (bf16[1024,1024]{1,0:T(8,128)(2,1)S(1)}, bf16[1024,1024]{1,0:T(8,128)(2,1)}, u32[]{:S(2)}) copy-start(bf16[1024,1024]{1,0:T(8,128)(2,1)} %param.14) | copy-start | bytes 6291460
  7.2 197.9 %all-gather.2.cloned.1.call-start = ((), (), s32[]{:S(2)}) async-start(), calls=%async_computation.2 | async-start | bytes 2654208 | tf_op jit(solution)/shard_map/all_gather | solution.py:148
  8.4 6.7 %collective-permute-start = (bf16[3,24,1024]{2,1,0:T(8,128)(2,1)S(1)}, bf16[3,24,1024]{2,1,0:T(8,128)(2,1)S(1)}, u32[]{:S(2)}, u32[]{:S(2)}) collective-permute-start(bf16[3,24,1024]{2,1,0:T(8,128)(2,1)S(1)} %get-tuple-element.25), channel_id=1, source_target_pairs={{0,8},{8,16},{16,24},{24,32},{32,40},{40,48},{48,56},{56,64},{64,7... | collective-permute-start | bytes 442376 | tf_op jit(solution)/shard_map/ppermute | solution.py:33
  12.0 7.2 %collective-permute-start.1 = (bf16[3,24,1024]{2,1,0:T(8,128)(2,1)S(1)}, bf16[3,24,1024]{2,1,0:T(8,128)(2,1)S(1)}, u32[]{:S(2)}, u32[]{:S(2)}) collective-permute-start(bf16[3,24,1024]{2,1,0:T(8,128)(2,1)S(1)} %get-tuple-element.24), channel_id=1, source_target_pairs={{8,0},{16,8},{24,16},{32,24},{40,32},{48,40},{56,48},{64,56},{72,6... | collective-permute-start | bytes 442376 | tf_op jit(solution)/shard_map/ppermute | solution.py:34
  19.2 6.3 %collective-permute-start.2 = (bf16[12,6,1024]{2,1,0:T(8,128)(2,1)S(1)}, bf16[12,6,1024]{2,1,0:T(8,128)(2,1)S(1)}, u32[]{:S(2)}, u32[]{:S(2)}) collective-permute-start(bf16[12,6,1024]{2,1,0:T(8,128)(2,1)S(1)} %get-tuple-element.22), channel_id=1, source_target_pairs={{0,1},{1,2},{2,3},{3,4},{4,5},{5,6},{6,7},{7,0},{8,9},{9,10},{10,1... | collective-permute-start | bytes 442376 | tf_op jit(solution)/shard_map/ppermute | solution.py:33
  19.3 6.3 %collective-permute-start.3 = (bf16[12,6,1024]{2,1,0:T(8,128)(2,1)S(1)}, bf16[12,6,1024]{2,1,0:T(8,128)(2,1)S(1)}, u32[]{:S(2)}, u32[]{:S(2)}) collective-permute-start(bf16[12,6,1024]{2,1,0:T(8,128)(2,1)S(1)} %get-tuple-element.23), channel_id=1, source_target_pairs={{1,0},{2,1},{3,2},{4,3},{5,4},{6,5},{7,6},{0,7},{9,8},{10,9},{11,1... | collective-permute-start | bytes 442376 | tf_op jit(solution)/shard_map/ppermute | solution.py:34
  27.9 4.5 %copy-start.10 = (f32[1024]{0:T(1024)S(1)}, f32[1024]{0:T(1024)}, u32[]{:S(2)}) copy-start(f32[1024]{0:T(1024)} %param.12) | copy-start | bytes 12292
  38.1 3.2 copy-start.4
  69.5 1.8 copy-start.8
  82.6 3.6 %copy-start.9 = (bf16[5,64,320]{2,1,0:T(8,128)(2,1)S(1)}, bf16[5,64,320]{2,1,0:T(8,128)(2,1)}, u32[]{:S(2)}) copy-start(bf16[5,64,320]{2,1,0:T(8,128)(2,1)} %param.17) | copy-start | bytes 614404
  82.6 84.4 %copy-start.13 = (s32[4]{0:T(128)S(1)}, s32[4]{0:T(128)}, u32[]{:S(2)}) copy-start(s32[4]{0:T(128)} %param.19) | copy-start | bytes 52
  82.6 84.4 %copy-start.14 = (s32[1,8]{1,0:T(1,128)S(1)}, s32[1,8]{1,0:T(1,128)}, u32[]{:S(2)}) copy-start(s32[1,8]{1,0:T(1,128)} %param.20) | copy-start | bytes 100
  82.6 95.8 %copy-start.15 = (s32[5]{0:T(128)S(1)}, s32[5]{0:T(128)}, u32[]{:S(2)}) copy-start(s32[5]{0:T(128)} %param.21) | copy-start | bytes 64
  86.1 175.6 %reduce-scatter.7.cloned.1.call-start = ((), (), s32[]{:S(2)}) async-start(), calls=%async_computation.4 | async-start | bytes 2654208
  86.4 15.6 %collective-permute-start.4 = (bf16[5,64,320]{1,2,0:T(8,128)(2,1)S(1)}, bf16[5,64,320]{1,2,0:T(8,128)(2,1)S(1)}, u32[]{:S(2)}, u32[]{:S(2)}) collective-permute-start(bf16[5,64,320]{1,2,0:T(8,128)(2,1)S(1)} %copy.70), channel_id=1, source_target_pairs={{0,8},{8,16},{16,24},{24,32},{32,40},{40,48},{48,56},{56,64},{64,7... | collective-permute-start | bytes 614408 | tf_op jit(solution)/shard_map/ppermute | solution.py:19
  88.0 13.9 %collective-permute-start.12 = (bf16[5,64,320]{1,2,0:T(8,128)(2,1)S(1)}, bf16[5,64,320]{1,2,0:T(8,128)(2,1)S(1)}, u32[]{:S(2)}, u32[]{:S(2)}) collective-permute-start(bf16[5,64,320]{1,2,0:T(8,128)(2,1)S(1)} %copy.70), channel_id=1, source_target_pairs={{0,120},{8,0},{16,8},{24,16},{32,24},{40,32},{48,40},{56,48},{64,5... | collective-permute-start | bytes 614408 | tf_op jit(solution)/shard_map/ppermute | solution.py:21
  102.0 14.7 %collective-permute-start.5 = (bf16[5,64,320]{1,2,0:T(8,128)(2,1)S(1)}, bf16[5,64,320]{1,2,0:T(8,128)(2,1)S(1)}, u32[]{:S(2)}, u32[]{:S(2)}) collective-permute-start(bf16[5,64,320]{1,2,0:T(8,128)(2,1)S(1)} %collective-permute-done.4), channel_id=1, source_target_pairs={{0,8},{8,16},{16,24},{24,32},{32,40},{40,48},{48,56},{56,64},{64,7... | collective-permute-start | bytes 614408 | tf_op jit(solution)/shard_map/ppermute | solution.py:19
  102.0 14.7 %collective-permute-start.13 = (bf16[5,64,320]{1,2,0:T(8,128)(2,1)S(1)}, bf16[5,64,320]{1,2,0:T(8,128)(2,1)S(1)}, u32[]{:S(2)}, u32[]{:S(2)}) collective-permute-start(bf16[5,64,320]{1,2,0:T(8,128)(2,1)S(1)} %collective-permute-done.12), channel_id=1, source_target_pairs={{0,120},{8,0},{16,8},{24,16},{32,24},{40,32},{48,40},{56,48},{64,5... | collective-permute-start | bytes 614408 | tf_op jit(solution)/shard_map/ppermute | solution.py:21
  116.6 13.8 %collective-permute-start.6 = (bf16[5,64,320]{1,2,0:T(8,128)(2,1)S(1)}, bf16[5,64,320]{1,2,0:T(8,128)(2,1)S(1)}, u32[]{:S(2)}, u32[]{:S(2)}) collective-permute-start(bf16[5,64,320]{1,2,0:T(8,128)(2,1)S(1)} %collective-permute-done.5), channel_id=1, source_target_pairs={{0,8},{8,16},{16,24},{24,32},{32,40},{40,48},{48,56},{56,64},{64,7... | collective-permute-start | bytes 614408 | tf_op jit(solution)/shard_map/ppermute | solution.py:19
  116.6 13.8 %collective-permute-start.14 = (bf16[5,64,320]{1,2,0:T(8,128)(2,1)S(1)}, bf16[5,64,320]{1,2,0:T(8,128)(2,1)S(1)}, u32[]{:S(2)}, u32[]{:S(2)}) collective-permute-start(bf16[5,64,320]{1,2,0:T(8,128)(2,1)S(1)} %collective-permute-done.13), channel_id=1, source_target_pairs={{0,120},{8,0},{16,8},{24,16},{32,24},{40,32},{48,40},{56,48},{64,5... | collective-permute-start | bytes 614408 | tf_op jit(solution)/shard_map/ppermute | solution.py:21
  130.4 12.9 %collective-permute-start.7 = (bf16[5,64,320]{1,2,0:T(8,128)(2,1)S(1)}, bf16[5,64,320]{1,2,0:T(8,128)(2,1)S(1)}, u32[]{:S(2)}, u32[]{:S(2)}) collective-permute-start(bf16[5,64,320]{1,2,0:T(8,128)(2,1)S(1)} %collective-permute-done.6), channel_id=1, source_target_pairs={{0,8},{8,16},{16,24},{24,32},{32,40},{40,48},{48,56},{56,64},{64,7... | collective-permute-start | bytes 614408 | tf_op jit(solution)/shard_map/ppermute | solution.py:19
  130.4 12.9 %collective-permute-start.15 = (bf16[5,64,320]{1,2,0:T(8,128)(2,1)S(1)}, bf16[5,64,320]{1,2,0:T(8,128)(2,1)}, u32[]{:S(2)}, u32[]{:S(2)}) collective-permute-start(bf16[5,64,320]{1,2,0:T(8,128)(2,1)S(1)} %collective-permute-done.14), channel_id=1, source_target_pairs={{0,120},{8,0},{16,8},{24,16},{32,24},{40,32},{48,40},{56,48},{64,5... | collective-permute-start | bytes 614408 | tf_op jit(solution)/shard_map/ppermute | solution.py:21
  143.3 12.1 %collective-permute-start.8 = (bf16[5,64,320]{1,2,0:T(8,128)(2,1)S(1)}, bf16[5,64,320]{1,2,0:T(8,128)(2,1)}, u32[]{:S(2)}, u32[]{:S(2)}) collective-permute-start(bf16[5,64,320]{1,2,0:T(8,128)(2,1)S(1)} %collective-permute-done.7), channel_id=1, source_target_pairs={{0,8},{8,16},{16,24},{24,32},{32,40},{40,48},{48,56},{56,64},{64,7... | collective-permute-start | bytes 614408 | tf_op jit(solution)/shard_map/ppermute | solution.py:19
  143.3 12.1 %collective-permute-start.16 = (bf16[5,64,320]{1,2,0:T(8,128)(2,1)}, bf16[5,64,320]{1,2,0:T(8,128)(2,1)}, u32[]{:S(2)}, u32[]{:S(2)}) collective-permute-start(bf16[5,64,320]{1,2,0:T(8,128)(2,1)} %collective-permute-done.15), channel_id=1, source_target_pairs={{0,120},{8,0},{16,8},{24,16},{32,24},{40,32},{48,40},{56,48},{64,5... | collective-permute-start | bytes 614408 | tf_op jit(solution)/shard_map/ppermute | solution.py:21
  155.4 11.6 %collective-permute-start.9 = (bf16[5,64,320]{1,2,0:T(8,128)(2,1)}, bf16[5,64,320]{1,2,0:T(8,128)(2,1)}, u32[]{:S(2)}, u32[]{:S(2)}) collective-permute-start(bf16[5,64,320]{1,2,0:T(8,128)(2,1)} %collective-permute-done.8), channel_id=1, source_target_pairs={{0,8},{8,16},{16,24},{24,32},{32,40},{40,48},{48,56},{56,64},{64,7... | collective-permute-start | bytes 614408 | tf_op jit(solution)/shard_map/ppermute | solution.py:19
  155.4 11.7 %collective-permute-start.17 = (bf16[5,64,320]{1,2,0:T(8,128)(2,1)}, bf16[5,64,320]{1,2,0:T(8,128)(2,1)S(1)}, u32[]{:S(2)}, u32[]{:S(2)}) collective-permute-start(bf16[5,64,320]{1,2,0:T(8,128)(2,1)} %collective-permute-done.16), channel_id=1, source_target_pairs={{0,120},{8,0},{16,8},{24,16},{32,24},{40,32},{48,40},{56,48},{64,5... | collective-permute-start | bytes 614408 | tf_op jit(solution)/shard_map/ppermute | solution.py:21
  166.9 11.5 %collective-permute-start.10 = (bf16[5,64,320]{1,2,0:T(8,128)(2,1)}, bf16[5,64,320]{1,2,0:T(8,128)(2,1)S(1)}, u32[]{:S(2)}, u32[]{:S(2)}) collective-permute-start(bf16[5,64,320]{1,2,0:T(8,128)(2,1)} %collective-permute-done.9), channel_id=1, source_target_pairs={{0,8},{8,16},{16,24},{24,32},{32,40},{40,48},{48,56},{56,64},{64,7... | collective-permute-start | bytes 614408 | tf_op jit(solution)/shard_map/ppermute | solution.py:19
  167.1 0.8 copy-start.5
  167.8 10.9 %collective-permute-start.18 = (bf16[5,64,320]{1,2,0:T(8,128)(2,1)S(1)}, bf16[5,64,320]{1,2,0:T(8,128)(2,1)S(1)}, u32[]{:S(2)}, u32[]{:S(2)}) collective-permute-start(bf16[5,64,320]{1,2,0:T(8,128)(2,1)S(1)} %collective-permute-done.17), channel_id=1, source_target_pairs={{0,120},{8,0},{16,8},{24,16},{32,24},{40,32},{48,40},{56,48},{64,5... | collective-permute-start | bytes 614408 | tf_op jit(solution)/shard_map/ppermute | solution.py:21
  178.4 0.8 copy-start.6
  178.4 11.4 %collective-permute-start.11 = (bf16[5,64,320]{1,2,0:T(8,128)(2,1)S(1)}, bf16[5,64,320]{1,2,0:T(8,128)(2,1)}, u32[]{:S(2)}, u32[]{:S(2)}) collective-permute-start(bf16[5,64,320]{1,2,0:T(8,128)(2,1)S(1)} %collective-permute-done.10), channel_id=1, source_target_pairs={{0,8},{8,16},{16,24},{24,32},{32,40},{40,48},{48,56},{56,64},{64,7... | collective-permute-start | bytes 614408 | tf_op jit(solution)/shard_map/ppermute | solution.py:19
  179.2 0.8 copy-start.7
  205.0 2.4 copy-start.11
  205.0 2.4 copy-start.12
  205.1 3.6 %copy-start.2 = (bf16[5,2048,320]{1,2,0:T(8,128)(2,1)S(1)}, bf16[5,2048,320]{1,2,0:T(8,128)(2,1)}, u32[]{:S(2)}) copy-start(bf16[5,2048,320]{1,2,0:T(8,128)(2,1)} %concatenate.14) | copy-start | bytes 19660804
  208.6 10.9 %copy-start.3 = (f32[6,192,1024]{2,1,0:T(8,128)}, f32[6,192,1024]{2,1,0:T(8,128)S(1)}, u32[]{:S(2)}) copy-start(f32[6,192,1024]{2,1,0:T(8,128)S(1)} %convert_element_type.67) | copy-start | bytes 14155780
  219.5 7.4 %copy-start.16 = (bf16[5,6,192,320]{3,2,1,0:T(8,128)(2,1)}, bf16[5,6,192,320]{3,2,1,0:T(8,128)(2,1)S(1)}, u32[]{:S(2)}) copy-start(bf16[5,6,192,320]{3,2,1,0:T(8,128)(2,1)S(1)} %multiply_convert_fusion) | copy-start | bytes 11059204
  228.6 116.4 %reduce-scatter.5.cloned.1.call-start = ((), (), s32[]{:S(2)}) async-start(), calls=%async_computation.3 | async-start | bytes 6684672 | tf_op jit(solution)/shard_map/reduce_scatter | solution.py:163
  246.1 100.8 %copy-start.1 = (bf16[1024,1024]{1,0:T(8,128)(2,1)S(1)}, bf16[1024,1024]{1,0:T(8,128)(2,1)}, u32[]{:S(2)}) copy-start(bf16[1024,1024]{1,0:T(8,128)(2,1)} %param.14) | copy-start | bytes 6291460
Sparse Core Ops, SparseCore 0:
  86.2 29.4 all-gather.1
  228.7 32.9 reduce-scatter.6
  265.2 79.8 reduce-scatter.4
